TPU v7x, 32 devices: a whole 2x2x4 slice. The times are simulated.
32 devices in a mesh: shard: 2 (over x), ctx: 4 (over z), tp: 4 (over y, core).
Axes of the slice: x: 2, y: 2, z: 4, core: 2. Of those that a mesh axis runs over, the one named last changes fastest.
Arguments:
- frames: bfloat16 [2, 2, 2048, 1280], P(None, 'shard', 'ctx'), may hold values from -6 to 6
- lengths: int32 [2, 2], P(None, 'shard'), may hold values from 0 to 2048, as said below
- first_gain: bfloat16 [1280], replicated, may hold values from 0.25 to 1.75
- first_bias: bfloat16 [1280], replicated, may hold values from -3 to 3
- query_weight: bfloat16 [1280, 1280], P('shard', 'tp'), may hold values from -0.15625 to 0.15625
- query_bias: bfloat16 [1280], P('tp'), may hold values from -3 to 3
- key_weight: bfloat16 [1280, 1280], P('shard', 'tp'), may hold values from -0.15625 to 0.15625
- value_weight: bfloat16 [1280, 1280], P('shard', 'tp'), may hold values from -0.15625 to 0.15625
- value_bias: bfloat16 [1280], P('tp'), may hold values from -0.088378906 to 0.088378906
- output_weight: bfloat16 [1280, 1280], P('shard', 'tp'), may hold values from -4 to 4
- output_bias: bfloat16 [1280], replicated, may hold values from -3 to 3
- second_gain: bfloat16 [1280], replicated, may hold values from 0.25 to 1.75
- second_bias: bfloat16 [1280], replicated, may hold values from -3 to 3
- inner_weight: bfloat16 [1280, 5120], P('shard', 'tp'), may hold values from -0.15625 to 0.15625
- inner_bias: bfloat16 [5120], P('tp'), may hold values from -3 to 3
- outer_weight: bfloat16 [1280, 5120], P('shard', 'tp'), may hold values from -0.15625 to 0.15625
- outer_bias: bfloat16 [1280], replicated, may hold values from -3 to 3
- cotangent: bfloat16 [2, 2, 2048, 1280], P(None, 'shard', 'ctx'), may hold values from -6 to 6
Outputs:
- result: bfloat16 [2, 2, 2048, 1280], P(None, 'shard', 'ctx')
- frames_grad: bfloat16 [2, 2, 2048, 1280], P(None, 'shard', 'ctx')
- first_gain_grad: float32 [1280], replicated
- first_bias_grad: float32 [1280], replicated
- query_weight_grad: float32 [1280, 1280], P('shard', 'tp')
- query_bias_grad: float32 [1280], P('tp')
- key_weight_grad: float32 [1280, 1280], P('shard', 'tp')
- value_weight_grad: float32 [1280, 1280], P('shard', 'tp')
- value_bias_grad: float32 [1280], P('tp')
- output_weight_grad: float32 [1280, 1280], P('shard', 'tp')
- output_bias_grad: float32 [1280], replicated
- second_gain_grad: float32 [1280], replicated
- second_bias_grad: float32 [1280], replicated
- inner_weight_grad: float32 [1280, 5120], P('shard', 'tp')
- inner_bias_grad: float32 [5120], P('tp')
- outer_weight_grad: float32 [1280, 5120], P('shard', 'tp')
- outer_bias_grad: float32 [1280], replicated
Inputs may be any that keep to these rules, and one draw needn't show every extreme that they name: Slot lengths count a clip's first frames; 0 marks an empty slot; in every draw some slot is empty and some slot is full.
All inputs are finite; a program needn't handle non-finite values.
Results may differ from a plain program's by a relative error of at most 0.025.
Values may be sent and summed in bfloat16 or wider, within the bound.
No kernel may reach another device: no remote copies, remote signals or barrier semaphores. Data moves between devices by JAX's collectives and lax.ppermute only.
A program may use at most 192 MiB of HBM per device.

v0:
```python
import math
import jax
import jax.numpy as jnp
from jax import lax
from jax.sharding import PartitionSpec as P

HD = 80
epsilon = 1e-05


def layer_norm(values, scale_gain, shift_bias):
    center = values - jnp.mean(values, -1, keepdims=True)
    spread = jnp.mean(center * center, -1, keepdims=True)
    return center * lax.rsqrt(spread + epsilon) * scale_gain + shift_bias


def per_device(
    frames,
    lengths,
    first_gain,
    first_bias,
    query_weight,
    query_bias,
    key_weight,
    value_weight,
    value_bias,
    output_weight,
    output_bias,
    second_gain,
    second_bias,
    inner_weight,
    inner_bias,
    outer_weight,
    outer_bias,
    cotangent,
):
    float_kind = jnp.float32
    half_kind = jnp.bfloat16
    batch_count = frames.shape[0]
    frame_rows = frames.shape[2]
    group_width = query_weight.shape[1]
    head_count = group_width // HD
    scaling = 1.0 / math.sqrt(HD)
    slot_frames = frame_rows * lax.axis_size("ctx")
    key_block = min(512, slot_frames)
    positions = lax.axis_index("ctx") * frame_rows + jnp.arange(frame_rows, dtype=jnp.int32)
    gain_one = first_gain.astype(float_kind)
    bias_one = first_bias.astype(float_kind)
    gain_two = second_gain.astype(float_kind)
    bias_two = second_bias.astype(float_kind)
    query_shift = query_bias.astype(float_kind)
    value_shift = value_bias.astype(float_kind)
    output_shift = output_bias.astype(float_kind)
    inner_shift = inner_bias.astype(float_kind)
    outer_shift = outer_bias.astype(float_kind)
    shards = (query_weight, key_weight, value_weight, output_weight, inner_weight, outer_weight)
    contract_last = (((1,), (1,)), ((), ()))
    contract_rows = (((0,), (0,)), ((), ()))
    results = []
    frame_grads = []
    small_totals = None
    weight_totals = None
    for batch_index in range(batch_count):
        gathered = (
            lax.all_gather(shards[0], "shard", axis=0, tiled=True),
            lax.all_gather(shards[1], "shard", axis=0, tiled=True),
            lax.all_gather(shards[2], "shard", axis=0, tiled=True),
            lax.all_gather(shards[3], "shard", axis=0, tiled=True),
            lax.all_gather(shards[4], "shard", axis=0, tiled=True),
            lax.all_gather(shards[5], "shard", axis=0, tiled=True),
        )
        full_query, full_key, full_value, full_output, full_inner, full_outer = gathered
        clip_frames = frames[batch_index, 0].astype(float_kind)
        length = lengths[batch_index, 0]
        frame_valid = positions < length
        has_frames = length > 0
        normed, first_back = jax.vjp(layer_norm, clip_frames, gain_one, bias_one)
        normed_low = normed.astype(half_kind)
        queries = (
            jnp.dot(normed_low, full_query, preferred_element_type=float_kind) + query_shift
        ).astype(half_kind)
        key_rows = jnp.dot(normed_low, full_key, preferred_element_type=float_kind).astype(
            half_kind
        )
        value_rows = (
            jnp.dot(normed_low, full_value, preferred_element_type=float_kind) + value_shift
        ).astype(half_kind)
        query_heads = queries.reshape(frame_rows, head_count, HD)
        start = jnp.int32(0)
        key_piece = lax.all_gather(key_rows, "ctx", axis=0, tiled=True)
        value_piece = lax.all_gather(value_rows, "ctx", axis=0, tiled=True)
        unnormal = jnp.zeros((frame_rows, head_count, HD), float_kind)
        weight_total = jnp.zeros((frame_rows, head_count), float_kind)
        piece_rows = key_piece.shape[0]
        for begin in range(0, piece_rows, key_block):
            count = min(key_block, piece_rows - begin)
            key_part = key_piece[begin : begin + count].reshape(count, head_count, HD)
            value_part = value_piece[begin : begin + count].reshape(count, head_count, HD)
            scores = (
                jnp.einsum("qhd,khd->hqk", query_heads, key_part, preferred_element_type=float_kind)
                * scaling
            )
            key_valid = start + begin + jnp.arange(count, dtype=jnp.int32) < length
            expo = jnp.where(key_valid[None, None, :], jnp.exp(scores), 0.0)
            weight_total = weight_total + jnp.sum(expo, -1).T
            unnormal = unnormal + jnp.einsum(
                "hqk,khd->qhd",
                expo.astype(half_kind),
                value_part,
                preferred_element_type=float_kind,
            )
        unnormal, weight_total = (unnormal, weight_total)
        denominator = jnp.where(has_frames, weight_total, 1.0)
        attended = unnormal / denominator[:, :, None]
        mixed_low = attended.reshape(frame_rows, group_width).astype(half_kind)
        partial_out = lax.dot_general(
            mixed_low, full_output, contract_last, preferred_element_type=float_kind
        )
        middle = (
            clip_frames
            + lax.psum(partial_out.astype(jnp.bfloat16), "tp").astype(jnp.float32)
            + output_shift
        )
        normed_two, second_back = jax.vjp(layer_norm, middle, gain_two, bias_two)
        normed_two_low = normed_two.astype(half_kind)
        inner_linear = (
            jnp.dot(normed_two_low, full_inner, preferred_element_type=float_kind) + inner_shift
        )
        activated, gelu_back = jax.vjp(
            lambda value_in: jax.nn.gelu(value_in, approximate=False), inner_linear
        )
        activated_low = activated.astype(half_kind)
        partial_ffn = lax.dot_general(
            activated_low, full_outer, contract_last, preferred_element_type=float_kind
        )
        final = (
            middle
            + lax.psum(partial_ffn.astype(jnp.bfloat16), "tp").astype(jnp.float32)
            + outer_shift
        )
        results.append(final.astype(half_kind))
        back_weights = (
            lax.all_gather(shards[0], "shard", axis=0, tiled=True),
            lax.all_gather(shards[1], "shard", axis=0, tiled=True),
            lax.all_gather(shards[2], "shard", axis=0, tiled=True),
            lax.all_gather(shards[3], "shard", axis=0, tiled=True),
            lax.all_gather(shards[4], "shard", axis=0, tiled=True),
            lax.all_gather(shards[5], "shard", axis=0, tiled=True),
        )
        back_query, back_key, back_value, back_output, back_inner, back_outer = back_weights
        grad_final = cotangent[batch_index, 0].astype(float_kind) * frame_valid[:, None].astype(
            float_kind
        )
        final_low = grad_final.astype(half_kind)
        grad_outer = lax.dot_general(
            final_low, activated_low, contract_rows, preferred_element_type=float_kind
        )
        grad_activated = jnp.dot(final_low, back_outer, preferred_element_type=float_kind)
        grad_inner = gelu_back(grad_activated)[0]
        inner_low = grad_inner.astype(half_kind)
        grad_inner_weight = lax.dot_general(
            normed_two_low, inner_low, contract_rows, preferred_element_type=float_kind
        )
        partial_two = lax.dot_general(
            inner_low, back_inner, contract_last, preferred_element_type=float_kind
        )
        grad_normed_two = lax.psum(partial_two.astype(jnp.bfloat16), "tp").astype(jnp.float32)
        grad_middle_norm, grad_gain_two, grad_bias_two = second_back(grad_normed_two)
        grad_middle = grad_final + grad_middle_norm
        middle_low = grad_middle.astype(half_kind)
        grad_output_weight = lax.dot_general(
            middle_low, mixed_low, contract_rows, preferred_element_type=float_kind
        )
        grad_attended = jnp.dot(middle_low, back_output, preferred_element_type=float_kind)
        grad_heads = grad_attended.reshape(frame_rows, head_count, HD)
        scaled_grad = (grad_heads / denominator[:, :, None]).astype(half_kind)
        delta_rows = (jnp.sum(grad_heads * attended, -1) / denominator).T
        all_keys, all_values = (
            lax.all_gather(key_rows, "ctx", axis=0, tiled=True),
            lax.all_gather(value_rows, "ctx", axis=0, tiled=True),
        )

        def key_step(grad_query, block_index):
            begin = block_index * key_block
            key_part = lax.dynamic_slice_in_dim(all_keys, begin, key_block, 0).reshape(
                key_block, head_count, HD
            )
            value_part = lax.dynamic_slice_in_dim(all_values, begin, key_block, 0).reshape(
                key_block, head_count, HD
            )
            scores = (
                jnp.einsum("qhd,khd->hqk", query_heads, key_part, preferred_element_type=float_kind)
                * scaling
            )
            key_valid = begin + jnp.arange(key_block, dtype=jnp.int32) < length
            expo = jnp.where(key_valid[None, None, :], jnp.exp(scores), 0.0)
            through_values = jnp.einsum(
                "qhd,khd->hqk", scaled_grad, value_part, preferred_element_type=float_kind
            )
            grad_scores = (scaling * expo * (through_values - delta_rows[:, :, None])).astype(
                half_kind
            )
            grad_query = grad_query + jnp.einsum(
                "hqk,khd->qhd", grad_scores, key_part, preferred_element_type=float_kind
            )
            key_term = jnp.einsum(
                "hqk,qhd->khd", grad_scores, query_heads, preferred_element_type=float_kind
            )
            value_term = jnp.einsum(
                "hqk,qhd->khd",
                expo.astype(half_kind),
                scaled_grad,
                preferred_element_type=float_kind,
            )
            return (grad_query, (key_term, value_term))

        grad_query, (key_terms, value_terms) = lax.scan(
            key_step,
            jnp.zeros((frame_rows, head_count, HD), float_kind),
            jnp.arange(slot_frames // key_block),
        )
        key_terms = key_terms.reshape(slot_frames, group_width)
        value_terms = value_terms.reshape(slot_frames, group_width)
        grad_keys, grad_values = (
            lax.psum_scatter(
                key_terms.astype(jnp.bfloat16), "ctx", scatter_dimension=0, tiled=True
            ).astype(jnp.float32),
            lax.psum_scatter(
                value_terms.astype(jnp.bfloat16), "ctx", scatter_dimension=0, tiled=True
            ).astype(jnp.float32),
        )
        query_low = grad_query.reshape(frame_rows, group_width).astype(half_kind)
        keys_low = grad_keys.astype(half_kind)
        values_low = grad_values.astype(half_kind)
        grad_query_weight = lax.dot_general(
            normed_low, query_low, contract_rows, preferred_element_type=float_kind
        )
        grad_key_weight = lax.dot_general(
            normed_low, keys_low, contract_rows, preferred_element_type=float_kind
        )
        grad_value_weight = lax.dot_general(
            normed_low, values_low, contract_rows, preferred_element_type=float_kind
        )
        partial_one = lax.dot_general(
            query_low, back_query, contract_last, preferred_element_type=float_kind
        )
        partial_one = partial_one + lax.dot_general(
            keys_low, back_key, contract_last, preferred_element_type=float_kind
        )
        partial_one = partial_one + lax.dot_general(
            values_low, back_value, contract_last, preferred_element_type=float_kind
        )
        grad_normed = lax.psum(partial_one.astype(jnp.bfloat16), "tp").astype(jnp.float32)
        grad_frames_norm, grad_gain_one, grad_bias_one = first_back(grad_normed)
        frame_grads.append((grad_middle + grad_frames_norm).astype(half_kind))
        small_terms = (
            grad_gain_one,
            grad_bias_one,
            jnp.sum(query_low.astype(float_kind), 0),
            jnp.sum(values_low.astype(float_kind), 0),
            jnp.sum(grad_middle, 0),
            grad_gain_two,
            grad_bias_two,
            jnp.sum(grad_inner, 0),
            jnp.sum(grad_final, 0),
        )
        small_totals = (
            small_terms
            if small_totals is None
            else jax.tree.map(jnp.add, small_totals, small_terms)
        )
        local_grads = (
            grad_query_weight,
            grad_key_weight,
            grad_value_weight,
            grad_output_weight,
            grad_inner_weight,
            grad_outer,
        )
        scattered = (
            lax.psum_scatter(
                local_grads[0].astype(jnp.bfloat16), "shard", scatter_dimension=0, tiled=True
            ).astype(jnp.float32),
            lax.psum_scatter(
                local_grads[1].astype(jnp.bfloat16), "shard", scatter_dimension=0, tiled=True
            ).astype(jnp.float32),
            lax.psum_scatter(
                local_grads[2].astype(jnp.bfloat16), "shard", scatter_dimension=0, tiled=True
            ).astype(jnp.float32),
            lax.psum_scatter(
                local_grads[3].astype(jnp.bfloat16), "shard", scatter_dimension=0, tiled=True
            ).astype(jnp.float32),
            lax.psum_scatter(
                local_grads[4].astype(jnp.bfloat16), "shard", scatter_dimension=0, tiled=True
            ).astype(jnp.float32),
            lax.psum_scatter(
                local_grads[5].astype(jnp.bfloat16), "shard", scatter_dimension=0, tiled=True
            ).astype(jnp.float32),
        )
        contribution = (
            lax.psum(scattered[0].astype(jnp.bfloat16), "ctx").astype(jnp.float32),
            lax.psum(scattered[1].astype(jnp.bfloat16), "ctx").astype(jnp.float32),
            lax.psum(scattered[2].astype(jnp.bfloat16), "ctx").astype(jnp.float32),
            lax.psum(scattered[3].astype(jnp.bfloat16), "ctx").astype(jnp.float32),
            lax.psum(scattered[4].astype(jnp.bfloat16), "ctx").astype(jnp.float32),
            lax.psum(scattered[5].astype(jnp.bfloat16), "ctx").astype(jnp.float32),
        )
        weight_totals = (
            contribution
            if weight_totals is None
            else jax.tree.map(jnp.add, weight_totals, contribution)
        )
    small_totals = lax.psum(small_totals, ("shard", "ctx"))
    return (
        jnp.stack(results)[:, None],
        jnp.stack(frame_grads)[:, None],
        small_totals[0],
        small_totals[1],
        weight_totals[0],
        small_totals[2],
        weight_totals[1],
        weight_totals[2],
        small_totals[3],
        weight_totals[3],
        small_totals[4],
        small_totals[5],
        small_totals[6],
        weight_totals[4],
        small_totals[7],
        weight_totals[5],
        small_totals[8],
    )


def solution(mesh):
    return jax.shard_map(
        per_device,
        mesh=mesh,
        in_specs=(
            P(None, "shard", "ctx", None),
            P(None, "shard"),
            P(),
            P(),
            P("shard", "tp"),
            P("tp"),
            P("shard", "tp"),
            P("shard", "tp"),
            P("tp"),
            P("shard", "tp"),
            P(),
            P(),
            P(),
            P("shard", "tp"),
            P("tp"),
            P("shard", "tp"),
            P(),
            P(None, "shard", "ctx", None),
        ),
        out_specs=(
            P(None, "shard", "ctx", None),
            P(None, "shard", "ctx", None),
            P(),
            P(),
            P("shard", "tp"),
            P("tp"),
            P("shard", "tp"),
            P("shard", "tp"),
            P("tp"),
            P("shard", "tp"),
            P(),
            P(),
            P(),
            P("shard", "tp"),
            P("tp"),
            P("shard", "tp"),
            P(),
        ),
        check_vma=False,
    )
```

profile of v0, /device:TPU:0, one launch (start us, length us, event | category | flops | bytes accessed | tf_op | source)
XLA Modules:
  0.0 1457.8 jit_solution(4725034005878868603)
XLA Ops:
  11.6 13.1 all_gather.23
  28.1 11.4 all_gather.20
  45.2 10.5 all_gather.22
  55.8 9.7 all_gather.25
  82.5 13.6 all-gather.7.cloned.1.call-done
  109.2 37.8 %all-reduce.10.cloned.1.call-done = bf16[512,1280]{1,0:T(8,128)(2,1)} async-done(((bf16[512,1280]{1,0:T(8,128)(2,1)}), bf16[512,1280]{1,0:T(8,128)(2,1)}) %all-reduce.10.cloned.1.call-update) | async-done | bytes 1310736 | tf_op jit(solution)/shard_map/psum | solution.py:121
  160.3 24.6 %all-gather.17.cloned.1.call-done = bf16[2048,320]{0,1:T(8,128)(2,1)} async-done(((bf16[512,320]{0,1:T(8,128)(2,1)}), bf16[2048,320]{0,1:T(8,128)(2,1)}) %all-gather.17.cloned.1.call-update) | async-done | bytes 1310736 | tf_op jit(solution)/shard_map/all_gather | solution.py:90
  190.2 28.3 %all-gather.15.cloned.1.call-done = bf16[2048,320]{0,1:T(8,128)(2,1)} async-done(((bf16[512,320]{0,1:T(8,128)(2,1)}), bf16[2048,320]{0,1:T(8,128)(2,1)}) %all-gather.15.cloned.1.call-update) | async-done | bytes 1310736 | tf_op jit(solution)/shard_map/all_gather | solution.py:91
  235.4 35.5 %all-reduce.12.cloned.1.call-done = bf16[512,1280]{1,0:T(8,128)(2,1)} async-done(((bf16[512,1280]{1,0:T(8,128)(2,1)}), bf16[512,1280]{1,0:T(8,128)(2,1)}) %all-reduce.12.cloned.1.call-update) | async-done | bytes 1310736 | tf_op jit(solution)/shard_map/psum | solution.py:121
  273.8 6.2 all-gather.11.cloned.1.call-done
  280.0 11.7 multiply_convert_fusion.3
  292.4 8.9 multiply_convert_fusion.2
  301.3 26.4 %all-gather.13.cloned.1.call-done = bf16[1280,1280]{1,0:T(8,128)(2,1)} async-done(((bf16[640,1280]{1,0:T(8,128)(2,1)}), bf16[1280,1280]{1,0:T(8,128)(2,1)}) %all-gather.13.cloned.1.call-update) | async-done | bytes 3276816 | tf_op jit(solution)/shard_map/all_gather | solution.py:70
  327.7 7.1 fusion.280
  347.2 60.0 %all-reduce.16.cloned.1.call-done = (bf16[512,1280]{1,0:T(8,128)(2,1)}, bf16[512,1280]{1,0:T(8,128)(2,1)}) async-done(((bf16[512,1280]{1,0:T(8,128)(2,1)}, bf16[512,1280]{1,0:T(8,128)(2,1)}), (bf16[512,1280]{1,0:T(8,128)(2,1)}, bf16[512,1280]{1,0:T(8,128)(2,1)})) %all-reduce.16.cloned.1.call-update) | async-done | bytes 2621456 | tf_op jit(solution)/shard_map/psum | solution.py:167
  423.3 60.1 %while.31 = (s32[]{:T(128)}, f32[512,4,80]{0,2,1:T(8,128)}, bf16[4,512,4,80]{1,3,2,0:T(8,128)(2,1)}, bf16[4,512,4,80]{1,3,2,0:T(8,128)(2,1)}, s32[4]{0:T(128)S(1...) while((s32[]{:T(128)}, f32[512,4,80]{0,2,1:T(8,128)}, ...), condition=%wide.region_36.37_spmd.clone, body=%wide.region_35.36_spmd.clone.sunk | while | flops 848626688 | bytes 52898636 | solution.py:217
  498.5 60.2 %while.30 = (s32[]{:T(128)}, f32[512,4,80]{0,2,1:T(8,128)}, bf16[4,512,4,80]{1,3,2,0:T(8,128)(2,1)}, bf16[4,512,4,80]{1,3,2,0:T(8,128)(2,1)}, s32[4]{0:T(128)S(1...) while((s32[]{:T(128)}, f32[512,4,80]{0,2,1:T(8,128)}, ...), condition=%wide.region_25.26_spmd.clone, body=%wide.region_24.25_spmd.clone.sunk | while | flops 848626688 | bytes 52898636 | solution.py:217
  597.3 29.0 %reduce-scatter.35.cloned.1.call-done = bf16[512,320]{0,1:T(8,128)(2,1)} async-done(((bf16[2048,320]{0,1:T(8,128)(2,1)}), bf16[512,320]{0,1:T(8,128)(2,1)}) %reduce-scatter.35.cloned.1.call-update) | async-done | bytes 327696 | tf_op jit(solution)/shard_map/reduce_scatter | solution.py:228
  673.4 17.1 %reduce-scatter.51.cloned.1.call-done = bf16[640,320]{1,0:T(8,128)(2,1)} async-done(((bf16[1280,320]{1,0:T(8,128)(2,1)}), bf16[640,320]{1,0:T(8,128)(2,1)}) %reduce-scatter.51.cloned.1.call-update) | async-done | bytes 409616
  692.5 19.9 %reduce-scatter.49.cloned.1.call-done = bf16[640,320]{1,0:T(8,128)(2,1)} async-done(((bf16[1280,320]{1,0:T(8,128)(2,1)}), bf16[640,320]{1,0:T(8,128)(2,1)}) %reduce-scatter.49.cloned.1.call-update) | async-done | bytes 409616
  714.3 19.9 %reduce-scatter.55.cloned.1.call-done = bf16[640,320]{1,0:T(8,128)(2,1)} async-done(((bf16[1280,320]{1,0:T(8,128)(2,1)}), bf16[640,320]{1,0:T(8,128)(2,1)}) %reduce-scatter.55.cloned.1.call-update) | async-done | bytes 409616
  736.2 19.9 %reduce-scatter.59.cloned.1.call-done = bf16[640,320]{1,0:T(8,128)(2,1)} async-done(((bf16[1280,320]{1,0:T(8,128)(2,1)}), bf16[640,320]{1,0:T(8,128)(2,1)}) %reduce-scatter.59.cloned.1.call-update) | async-done | bytes 409616
  758.0 19.9 %reduce-scatter.53.cloned.1.call-done = bf16[640,320]{1,0:T(8,128)(2,1)} async-done(((bf16[1280,320]{1,0:T(8,128)(2,1)}), bf16[640,320]{1,0:T(8,128)(2,1)}) %reduce-scatter.53.cloned.1.call-update) | async-done | bytes 409616
  779.8 20.0 %reduce-scatter.57.cloned.1.call-done = bf16[640,320]{1,0:T(8,128)(2,1)} async-done(((bf16[1280,320]{1,0:T(8,128)(2,1)}), bf16[640,320]{1,0:T(8,128)(2,1)}) %reduce-scatter.57.cloned.1.call-update) | async-done | bytes 409616
  801.8 45.6 %reduce-scatter.41.cloned.1.call-done = bf16[640,1280]{1,0:T(8,128)(2,1)} async-done(((bf16[1280,1280]{1,0:T(8,128)(2,1)}), bf16[640,1280]{1,0:T(8,128)(2,1)}) %reduce-scatter.41.cloned.1.call-update) | async-done | bytes 1638416 | tf_op jit(solution)/shard_map/reduce_scatter | solution.py:293
  847.4 47.7 %reduce-scatter.43.cloned.1.call-done = bf16[640,1280]{1,0:T(8,128)(2,1)} async-done(((bf16[1280,1280]{1,0:T(8,128)(2,1)}), bf16[640,1280]{1,0:T(8,128)(2,1)}) %reduce-scatter.43.cloned.1.call-update) | async-done | bytes 1638416 | tf_op jit(solution)/shard_map/reduce_scatter | solution.py:293
  895.1 47.2 %reduce-scatter.45.cloned.1.call-done = bf16[640,1280]{1,0:T(8,128)(2,1)} async-done(((bf16[1280,1280]{1,0:T(8,128)(2,1)}), bf16[640,1280]{1,0:T(8,128)(2,1)}) %reduce-scatter.45.cloned.1.call-update) | async-done | bytes 1638416 | tf_op jit(solution)/shard_map/reduce_scatter | solution.py:296
  942.3 47.2 %reduce-scatter.47.cloned.1.call-done = bf16[640,1280]{1,0:T(8,128)(2,1)} async-done(((bf16[1280,1280]{1,0:T(8,128)(2,1)}), bf16[640,1280]{1,0:T(8,128)(2,1)}) %reduce-scatter.47.cloned.1.call-update) | async-done | bytes 1638416 | tf_op jit(solution)/shard_map/reduce_scatter | solution.py:296
  990.7 103.8 %all-reduce.14.cloned.1.call-done = (bf16[512,1280]{1,0:T(8,128)(2,1)}, bf16[512,1280]{1,0:T(8,128)(2,1)}, bf16[512,1280]{1,0:T(8,128)(2,1)}, bf16[512,1280]{1,0:T(8,128)(2,1)}) async-done(((bf16[512,1280]{1,0:T(8,128)(2,1)}, bf16[512,1280]{1,0:T(8,128)(2,1)}, bf16[512,1280]{1,0:T(8,128)(2,1)}, bf16[512,1280]{1,0:T(8,128)(2,1)}), (bf16[512,1280]{1,0:T(8,128)(2,1)}, bf16[512,1280]{1,0:T(8,128)(2,1)}, ...) | async-done | bytes 5242896 | tf_op jit(solution)/shard_map/psum | solution.py:138
  1098.1 6.3 fusion.93
  1104.4 41.7 %all-reduce = (f32[1280]{0:T(1024)}, f32[1280]{0:T(1024)}, f32[320]{0:T(512)}, f32[320]{0:T(512)}, f32[1280]{0:T(1024)}, /*index=5*/f32[1280]{0:T(1024)}, f32[1280]{0:T(1024)}, f32[1280]{0:T(1024)}, f32[1280]{0:T(1024)}) all-reduce(f32[1280]{0:T(1024)S(1)} %add.526, ...), channel_id=1, replica_groups=mesh['shard'=2,'ctx'=4,'tp'=4] {'shard','ctx'}, use_global_device_ids=true, to_apply=%region_44.45 | all-reduce | flops 9600 | bytes 76800 | tf_op jit(solution)/shard_map/psum | solution.py:313
  1154.9 285.4 %all-reduce.18.cloned.1.call-done = (bf16[640,320]{0,1:T(8,128)(2,1)}, bf16[640,320]{0,1:T(8,128)(2,1)}, bf16[640,320]{0,1:T(8,128)(2,1)}, bf16[640,320]{0,1:T(8...) async-done(((bf16[640,320]{0,1:T(8,128)(2,1)}, ...) | async-done | bytes 9830416 | tf_op jit(solution)/shard_map/psum | solution.py:301
  (566 shorter events, 358.3 us)
Async XLA Ops:
  8.1 60.9 %all-gather.9.cloned.1.call-start = ((), (), s32[]{:S(2)}) async-start(), calls=%async_computation.17 | async-start | bytes 1638400 | tf_op jit(solution)/shard_map/all_gather | solution.py:90
  11.1 138.1 %copy-start.73 = (f32[1280]{0:T(1024)}, f32[1280]{0:T(1024)S(1)}, u32[]{:S(2)}) copy-start(f32[1280]{0:T(1024)S(1)} %convert_element_type.409) | copy-start | bytes 15364
  11.6 137.6 %copy-start.75 = (f32[1280]{0:T(1024)}, f32[1280]{0:T(1024)S(1)}, u32[]{:S(2)}) copy-start(f32[1280]{0:T(1024)S(1)} %convert_element_type.410) | copy-start | bytes 15364
  28.1 68.0 %all-gather.7.cloned.1.call-start = ((), (), s32[]{:S(2)}) async-start(), calls=%async_computation.16 | async-start | bytes 1638400 | tf_op jit(solution)/shard_map/all_gather | solution.py:91
  43.2 103.8 %all-reduce.10.cloned.1.call-start = ((), (), s32[]{:S(2)}) async-start(), calls=%async_computation.18 | async-start | bytes 2621440 | tf_op jit(solution)/shard_map/psum | solution.py:121
  108.6 76.3 %all-gather.17.cloned.1.call-start = ((), (), s32[]{:S(2)}) async-start(), calls=%async_computation.22 | async-start | bytes 1638400 | tf_op jit(solution)/shard_map/all_gather | solution.py:90
  109.2 40.6 %copy-start.79 = (f32[512]{0:T(512)}, f32[512]{0:T(512)S(1)}, u32[]{:S(2)}) copy-start(f32[512]{0:T(512)S(1)} %broadcast_multiply_fusion.1) | copy-start | bytes 6148
  109.2 41.7 %copy-start.25 = (bf16[1280,320]{0,1:T(8,128)(2,1)S(1)}, bf16[1280,320]{0,1:T(8,128)(2,1)}, u32[]{:S(2)}) copy-start(bf16[1280,320]{0,1:T(8,128)(2,1)} %copy-done.24) | copy-start | bytes 2457604
  152.2 66.3 %all-gather.15.cloned.1.call-start = ((), (), s32[]{:S(2)}) async-start(), calls=%async_computation.21 | async-start | bytes 1638400 | tf_op jit(solution)/shard_map/all_gather | solution.py:91
  155.2 115.7 %all-reduce.12.cloned.1.call-start = ((), (), s32[]{:S(2)}) async-start(), calls=%async_computation.23 | async-start | bytes 2621440 | tf_op jit(solution)/shard_map/psum | solution.py:121
  232.6 47.4 %all-gather.11.cloned.1.call-start = ((), (), s32[]{:S(2)}) async-start(), calls=%async_computation.19 | async-start | bytes 4915200 | tf_op jit(solution)/shard_map/all_gather | solution.py:69
  233.1 94.5 %all-gather.13.cloned.1.call-start = ((), (), s32[]{:S(2)}) async-start(), calls=%async_computation.20 | async-start | bytes 4915200 | tf_op jit(solution)/shard_map/all_gather | solution.py:70
  233.7 173.5 %all-reduce.16.cloned.1.call-start = ((), (), s32[]{:S(2)}) async-start(), calls=%async_computation.41 | async-start | bytes 5242880 | tf_op jit(solution)/shard_map/psum | solution.py:167
  235.4 57.0 %copy-start.95 = (f32[1280]{0:T(1024)}, f32[1280]{0:T(1024)S(1)}, u32[]{:S(2)}) copy-start(f32[1280]{0:T(1024)S(1)} %convert_element_type.427) | copy-start | bytes 15364
  347.1 237.2 %reduce-scatter.37.cloned.1.call-start = ((), (), s32[]{:S(2)}) async-start(), calls=%async_computation.26 | async-start | bytes 1638400 | tf_op jit(solution)/shard_map/reduce_scatter | solution.py:225
  487.2 100.7 %reduce-scatter.39.cloned.1.call-start = ((), (), s32[]{:S(2)}) async-start(), calls=%async_computation.27 | async-start | bytes 1638400 | tf_op jit(solution)/shard_map/reduce_scatter | solution.py:228
  496.0 97.8 %reduce-scatter.33.cloned.1.call-start = ((), (), s32[]{:S(2)}) async-start(), calls=%async_computation.24 | async-start | bytes 1638400 | tf_op jit(solution)/shard_map/reduce_scatter | solution.py:225
  562.5 63.8 %reduce-scatter.35.cloned.1.call-start = ((), (), s32[]{:S(2)}) async-start(), calls=%async_computation.25 | async-start | bytes 1638400 | tf_op jit(solution)/shard_map/reduce_scatter | solution.py:228
  566.3 103.1 %reduce-scatter.63.cloned.1.call-start = ((), (), s32[]{:S(2)}) async-start(), calls=%async_computation.39 | async-start | bytes 1474560
  570.2 101.3 %reduce-scatter.61.cloned.1.call-start = ((), (), s32[]{:S(2)}) async-start(), calls=%async_computation.38 | async-start | bytes 1474560
  575.9 114.6 %reduce-scatter.51.cloned.1.call-start = ((), (), s32[]{:S(2)}) async-start(), calls=%async_computation.33 | async-start | bytes 1474560
  580.9 131.4 %reduce-scatter.49.cloned.1.call-start = ((), (), s32[]{:S(2)}) async-start(), calls=%async_computation.32 | async-start | bytes 1474560
  584.3 149.9 %reduce-scatter.55.cloned.1.call-start = ((), (), s32[]{:S(2)}) async-start(), calls=%async_computation.35 | async-start | bytes 1474560
  587.8 168.3 %reduce-scatter.59.cloned.1.call-start = ((), (), s32[]{:S(2)}) async-start(), calls=%async_computation.37 | async-start | bytes 1474560
  591.2 186.7 %reduce-scatter.53.cloned.1.call-start = ((), (), s32[]{:S(2)}) async-start(), calls=%async_computation.34 | async-start | bytes 1474560
  597.2 202.6 %reduce-scatter.57.cloned.1.call-start = ((), (), s32[]{:S(2)}) async-start(), calls=%async_computation.36 | async-start | bytes 1474560
  629.6 217.8 %reduce-scatter.41.cloned.1.call-start = ((), (), s32[]{:S(2)}) async-start(), calls=%async_computation.28 | async-start | bytes 4915200 | tf_op jit(solution)/shard_map/reduce_scatter | solution.py:293
  635.2 259.9 %reduce-scatter.43.cloned.1.call-start = ((), (), s32[]{:S(2)}) async-start(), calls=%async_computation.29 | async-start | bytes 4915200 | tf_op jit(solution)/shard_map/reduce_scatter | solution.py:293
  640.8 301.5 %reduce-scatter.45.cloned.1.call-start = ((), (), s32[]{:S(2)}) async-start(), calls=%async_computation.30 | async-start | bytes 4915200 | tf_op jit(solution)/shard_map/reduce_scatter | solution.py:296
  646.4 343.1 %reduce-scatter.47.cloned.1.call-start = ((), (), s32[]{:S(2)}) async-start(), calls=%async_computation.31 | async-start | bytes 4915200 | tf_op jit(solution)/shard_map/reduce_scatter | solution.py:296
  651.9 442.6 %all-reduce.14.cloned.1.call-start = ((), (), s32[]{:S(2)}) async-start(), calls=%async_computation.40 | async-start | bytes 10485760 | tf_op jit(solution)/shard_map/psum | solution.py:138
  669.2 771.1 %all-reduce.18.cloned.1.call-start = ((), (), s32[]{:S(2)}) async-start(), calls=%async_computation.42 | async-start | bytes 19660800 | tf_op jit(solution)/shard_map/psum | solution.py:301
  (136 other events, 484.6 us)
Sparse Core Ops, SparseCore 0:
  28.2 33.9 all-gather.8
  64.3 31.6 all-gather.6
  108.7 38.2 all-reduce.9
  152.4 32.5 all-gather.16
  186.9 31.6 all-gather.14
  232.7 38.2 all-reduce.11
  347.2 59.9 all-reduce.15
  487.3 31.4 reduce-scatter.36
  521.7 30.0 reduce-scatter.38
  562.6 31.2 reduce-scatter.32
  596.2 30.0 reduce-scatter.34
  628.4 18.3 reduce-scatter.62
  649.0 19.6 reduce-scatter.60
  670.8 19.6 reduce-scatter.50
  692.6 19.6 reduce-scatter.48
  714.5 19.6 reduce-scatter.54
  736.3 19.6 reduce-scatter.58
  758.1 19.6 reduce-scatter.52
  780.1 19.6 reduce-scatter.56
  802.5 44.8 reduce-scatter.40
  850.2 44.8 reduce-scatter.42
  897.4 44.8 reduce-scatter.44
  944.6 44.8 reduce-scatter.46
  991.9 102.5 all-reduce.13
  1099.9 340.3 all-reduce.17
Sparse Core Ops, SparseCore 1:
  234.6 45.3 all-gather.10
  281.4 46.2 all-gather.12
where the time goes:
time: 1470 us; the launch traced here: 1460 us
  waiting for transfers between devices  959 us (65%)
  matrix products  225 us (15%)
  local copies, waits for them, and re-layouts  97 us (7%)
  blocking collectives  86.5 us (6%)
  other arithmetic  63.9 us (4%)
  between operations  18.4 us (1%)
    psum x1, waiting for transfers between devices, per_device(): lax.psum(scattered[0].astype(jnp.bfloat16), 'ctx').astype(jnp.float32)  285 us
    unnamed x35, waiting for transfers between devices  118 us
    psum x1, waiting for transfers between devices, per_device(): lax.psum(partial_ffn.astype(jnp.bfloat16), 'tp').astype(jnp.float32)  104 us
    reduce_scatter x2, waiting for transfers between devices, per_device(): lax.psum_scatter(local_grads[5].astype(jnp.bfloat16), 'shard', scatter_di...  94.3 us
    reduce_scatter x2, waiting for transfers between devices, per_device(): lax.psum_scatter(local_grads[4].astype(jnp.bfloat16), 'shard', scatter_di...  93.3 us
    psum x2, waiting for transfers between devices, per_device(): lax.psum(partial_out.astype(jnp.bfloat16), 'tp').astype(jnp.float32)  73.4 us
    psum x1, waiting for transfers between devices, per_device(): lax.psum(partial_two.astype(jnp.bfloat16), 'tp').astype(jnp.float32)  60 us
    unnamed x238, local copies, waits for them, and re-layouts  51.3 us
  transfers between devices with their start and end apart: 27, of which 22 were waited for; matrix products, arithmetic and copies ran while one was open for 16% of the time, Pallas kernels for 0%

commit v1 on v0

--- a/solution.py
+++ b/solution.py
@@ -116,9 +116,13 @@
         partial_out = lax.dot_general(
             mixed_low, full_output, contract_last, preferred_element_type=float_kind
         )
+
+        def register_scenes_for(block_in, group_axis):
+            return jax.lax.all_gather(block_in, group_axis).sum(axis=0)
+
         middle = (
             clip_frames
-            + lax.psum(partial_out.astype(jnp.bfloat16), "tp").astype(jnp.float32)
+            + register_scenes_for(partial_out.astype(jnp.bfloat16), "tp").astype(jnp.float32)
             + output_shift
         )
         normed_two, second_back = jax.vjp(layer_norm, middle, gain_two, bias_two)

time: 1470 us -> 1510 us (1.027)
  waiting for transfers between devices: 959 us -> 997 us
    all_gather x0 -> x2, waiting for transfers between devices: none -> 75.8 us  [register_scenes_for(): return jax.lax.all_gather(block_in, group_axis).sum(axis=0)]
    psum x2 -> x0, waiting for transfers between devices: 73.4 us -> none  [per_device(): lax.psum(partial_out.astype(jnp.bfloat16), 'tp').astype(jnp.float32)]
    all_gather x1, waiting for transfers between devices: 6.2 us -> 40.4 us  [per_device(): lax.all_gather(shards[4], 'shard', axis=0, tiled=True)]
    unnamed x238 -> x240, local copies, waits for them, and re-layouts: 51.3 us -> 51.3 us
where the time goes in v1:
time: 1510 us; the launch traced here: 1500 us
  waiting for transfers between devices  997 us (66%)
  matrix products  225 us (15%)
  local copies, waits for them, and re-layouts  96.9 us (6%)
  blocking collectives  86.6 us (6%)
  other arithmetic  72.6 us (5%)
  between operations  17.2 us (1%)
    psum x1, waiting for transfers between devices, per_device(): lax.psum(scattered[0].astype(jnp.bfloat16), 'ctx').astype(jnp.float32)  285 us
    unnamed x35, waiting for transfers between devices  118 us
    psum x1, waiting for transfers between devices, per_device(): lax.psum(partial_ffn.astype(jnp.bfloat16), 'tp').astype(jnp.float32)  104 us
    reduce_scatter x2, waiting for transfers between devices, per_device(): lax.psum_scatter(local_grads[5].astype(jnp.bfloat16), 'shard', scatter_di...  94.1 us
    reduce_scatter x2, waiting for transfers between devices, per_device(): lax.psum_scatter(local_grads[4].astype(jnp.bfloat16), 'shard', scatter_di...  93.5 us
    all_gather x2, waiting for transfers between devices, register_scenes_for(): return jax.lax.all_gather(block_in, group_axis).sum(axis=0)  75.8 us
    psum x1, waiting for transfers between devices, per_device(): lax.psum(partial_two.astype(jnp.bfloat16), 'tp').astype(jnp.float32)  60 us
    unnamed x240, local copies, waits for them, and re-layouts  51.3 us
  transfers between devices with their start and end apart: 27, of which 22 were waited for; matrix products, arithmetic and copies ran while one was open for 16% of the time, Pallas kernels for 0%

profile of v1, /device:TPU:0, one launch (start us, length us, event | category | flops | bytes accessed | tf_op | source)
XLA Modules:
  0.0 1502.7 jit_solution(2736862184695648874)
XLA Ops:
  10.8 13.1 all_gather.31
  27.3 11.4 all_gather.28
  44.4 10.5 all_gather.30
  55.0 9.7 all_gather.33
  82.1 13.1 all-gather.11.cloned.1.call-done
  108.3 39.2 %all-gather.23.cloned.1.call-done = bf16[2048,1280]{1,0:T(8,128)(2,1)} async-done(((bf16[512,1280]{1,0:T(8,128)(2,1)}), bf16[2048,1280]{1,0:T(8,128)(2,1)}) %all-gather.23.cloned.1.call-update) | async-done | bytes 5242896 | tf_op jit(solution)/shard_map/all_gather | solution.py:121
  164.7 25.5 %all-gather.21.cloned.1.call-done = bf16[2048,320]{0,1:T(8,128)(2,1)} async-done(((bf16[512,320]{0,1:T(8,128)(2,1)}), bf16[2048,320]{0,1:T(8,128)(2,1)}) %all-gather.21.cloned.1.call-update) | async-done | bytes 1310736 | tf_op jit(solution)/shard_map/all_gather | solution.py:90
  195.4 28.4 %all-gather.19.cloned.1.call-done = bf16[2048,320]{0,1:T(8,128)(2,1)} async-done(((bf16[512,320]{0,1:T(8,128)(2,1)}), bf16[2048,320]{0,1:T(8,128)(2,1)}) %all-gather.19.cloned.1.call-update) | async-done | bytes 1310736 | tf_op jit(solution)/shard_map/all_gather | solution.py:91
  240.9 36.6 %all-gather.25.cloned.1.call-done = bf16[2048,1280]{1,0:T(8,128)(2,1)} async-done(((bf16[512,1280]{1,0:T(8,128)(2,1)}), bf16[2048,1280]{1,0:T(8,128)(2,1)}) %all-gather.25.cloned.1.call-update) | async-done | bytes 5242896 | tf_op jit(solution)/shard_map/all_gather | solution.py:121
  285.0 40.4 %all-gather.15.cloned.1.call-done = bf16[1280,1280]{1,0:T(8,128)(2,1)} async-done(((bf16[640,1280]{1,0:T(8,128)(2,1)}), bf16[1280,1280]{1,0:T(8,128)(2,1)}) %all-gather.15.cloned.1.call-update) | async-done | bytes 3276816 | tf_op jit(solution)/shard_map/all_gather | solution.py:69
  325.4 11.7 multiply_convert_fusion.3
  337.8 8.9 multiply_convert_fusion.2
  346.7 26.7 %all-gather.17.cloned.1.call-done = bf16[1280,1280]{1,0:T(8,128)(2,1)} async-done(((bf16[640,1280]{1,0:T(8,128)(2,1)}), bf16[1280,1280]{1,0:T(8,128)(2,1)}) %all-gather.17.cloned.1.call-update) | async-done | bytes 3276816 | tf_op jit(solution)/shard_map/all_gather | solution.py:70
  373.4 7.1 fusion.280
  392.9 60.0 %all-reduce.10.cloned.1.call-done = (bf16[512,1280]{1,0:T(8,128)(2,1)}, bf16[512,1280]{1,0:T(8,128)(2,1)}) async-done(((bf16[512,1280]{1,0:T(8,128)(2,1)}, bf16[512,1280]{1,0:T(8,128)(2,1)}), (bf16[512,1280]{1,0:T(8,128)(2,1)}, bf16[512,1280]{1,0:T(8,128)(2,1)})) %all-reduce.10.cloned.1.call-update) | async-done | bytes 2621456 | tf_op jit(solution)/shard_map/psum | solution.py:171
  468.9 59.5 %while.31 = (s32[]{:T(128)}, f32[512,4,80]{0,2,1:T(8,128)}, bf16[4,512,4,80]{1,3,2,0:T(8,128)(2,1)}, bf16[4,512,4,80]{1,3,2,0:T(8,128)(2,1)}, s32[4]{0:T(128)S(1...) while((s32[]{:T(128)}, f32[512,4,80]{0,2,1:T(8,128)}, ...), condition=%wide.region_36.37_spmd.clone, body=%wide.region_35.36_spmd.clone.sunk | while | flops 848626688 | bytes 52898636 | solution.py:221
  543.5 60.4 %while.30 = (s32[]{:T(128)}, f32[512,4,80]{0,2,1:T(8,128)}, bf16[4,512,4,80]{1,3,2,0:T(8,128)(2,1)}, bf16[4,512,4,80]{1,3,2,0:T(8,128)(2,1)}, s32[4]{0:T(128)S(1...) while((s32[]{:T(128)}, f32[512,4,80]{0,2,1:T(8,128)}, ...), condition=%wide.region_25.26_spmd.clone, body=%wide.region_24.25_spmd.clone.sunk | while | flops 848626688 | bytes 52898636 | solution.py:221
  642.5 29.0 %reduce-scatter.35.cloned.1.call-done = bf16[512,320]{0,1:T(8,128)(2,1)} async-done(((bf16[2048,320]{0,1:T(8,128)(2,1)}), bf16[512,320]{0,1:T(8,128)(2,1)}) %reduce-scatter.35.cloned.1.call-update) | async-done | bytes 327696 | tf_op jit(solution)/shard_map/reduce_scatter | solution.py:232
  718.7 17.0 %reduce-scatter.51.cloned.1.call-done = bf16[640,320]{1,0:T(8,128)(2,1)} async-done(((bf16[1280,320]{1,0:T(8,128)(2,1)}), bf16[640,320]{1,0:T(8,128)(2,1)}) %reduce-scatter.51.cloned.1.call-update) | async-done | bytes 409616
  737.6 19.9 %reduce-scatter.49.cloned.1.call-done = bf16[640,320]{1,0:T(8,128)(2,1)} async-done(((bf16[1280,320]{1,0:T(8,128)(2,1)}), bf16[640,320]{1,0:T(8,128)(2,1)}) %reduce-scatter.49.cloned.1.call-update) | async-done | bytes 409616
  759.4 19.9 %reduce-scatter.55.cloned.1.call-done = bf16[640,320]{1,0:T(8,128)(2,1)} async-done(((bf16[1280,320]{1,0:T(8,128)(2,1)}), bf16[640,320]{1,0:T(8,128)(2,1)}) %reduce-scatter.55.cloned.1.call-update) | async-done | bytes 409616
  781.3 20.0 %reduce-scatter.59.cloned.1.call-done = bf16[640,320]{1,0:T(8,128)(2,1)} async-done(((bf16[1280,320]{1,0:T(8,128)(2,1)}), bf16[640,320]{1,0:T(8,128)(2,1)}) %reduce-scatter.59.cloned.1.call-update) | async-done | bytes 409616
  803.3 19.8 %reduce-scatter.53.cloned.1.call-done = bf16[640,320]{1,0:T(8,128)(2,1)} async-done(((bf16[1280,320]{1,0:T(8,128)(2,1)}), bf16[640,320]{1,0:T(8,128)(2,1)}) %reduce-scatter.53.cloned.1.call-update) | async-done | bytes 409616
  825.1 20.0 %reduce-scatter.57.cloned.1.call-done = bf16[640,320]{1,0:T(8,128)(2,1)} async-done(((bf16[1280,320]{1,0:T(8,128)(2,1)}), bf16[640,320]{1,0:T(8,128)(2,1)}) %reduce-scatter.57.cloned.1.call-update) | async-done | bytes 409616
  847.1 45.7 %reduce-scatter.41.cloned.1.call-done = bf16[640,1280]{1,0:T(8,128)(2,1)} async-done(((bf16[1280,1280]{1,0:T(8,128)(2,1)}), bf16[640,1280]{1,0:T(8,128)(2,1)}) %reduce-scatter.41.cloned.1.call-update) | async-done | bytes 1638416 | tf_op jit(solution)/shard_map/reduce_scatter | solution.py:297
  892.8 47.7 %reduce-scatter.43.cloned.1.call-done = bf16[640,1280]{1,0:T(8,128)(2,1)} async-done(((bf16[1280,1280]{1,0:T(8,128)(2,1)}), bf16[640,1280]{1,0:T(8,128)(2,1)}) %reduce-scatter.43.cloned.1.call-update) | async-done | bytes 1638416 | tf_op jit(solution)/shard_map/reduce_scatter | solution.py:297
  940.5 47.0 %reduce-scatter.45.cloned.1.call-done = bf16[640,1280]{1,0:T(8,128)(2,1)} async-done(((bf16[1280,1280]{1,0:T(8,128)(2,1)}), bf16[640,1280]{1,0:T(8,128)(2,1)}) %reduce-scatter.45.cloned.1.call-update) | async-done | bytes 1638416 | tf_op jit(solution)/shard_map/reduce_scatter | solution.py:300
  987.5 47.1 %reduce-scatter.47.cloned.1.call-done = bf16[640,1280]{1,0:T(8,128)(2,1)} async-done(((bf16[1280,1280]{1,0:T(8,128)(2,1)}), bf16[640,1280]{1,0:T(8,128)(2,1)}) %reduce-scatter.47.cloned.1.call-update) | async-done | bytes 1638416 | tf_op jit(solution)/shard_map/reduce_scatter | solution.py:300
  1035.9 103.8 %all-reduce.8.cloned.1.call-done = (bf16[512,1280]{1,0:T(8,128)(2,1)}, bf16[512,1280]{1,0:T(8,128)(2,1)}, bf16[512,1280]{1,0:T(8,128)(2,1)}, bf16[512,1280]{1,0:T(8,128)(2,1)}) async-done(((bf16[512,1280]{1,0:T(8,128)(2,1)}, bf16[512,1280]{1,0:T(8,128)(2,1)}, bf16[512,1280]{1,0:T(8,128)(2,1)}, bf16[512,1280]{1,0:T(8,128)(2,1)}), (bf16[512,1280]{1,0:T(8,128)(2,1)}, bf16[512,1280]{1,0:T(8,128)(2,1)}, ...) | async-done | bytes 5242896 | tf_op jit(solution)/shard_map/psum | solution.py:142
  1143.3 6.3 fusion.93
  1149.7 41.8 %all-reduce = (f32[1280]{0:T(1024)}, f32[1280]{0:T(1024)}, f32[320]{0:T(512)}, f32[320]{0:T(512)}, f32[1280]{0:T(1024)}, /*index=5*/f32[1280]{0:T(1024)}, f32[1280]{0:T(1024)}, f32[1280]{0:T(1024)}, f32[1280]{0:T(1024)}) all-reduce(f32[1280]{0:T(1024)S(1)} %add.522, ...), channel_id=1, replica_groups=mesh['shard'=2,'ctx'=4,'tp'=4] {'shard','ctx'}, use_global_device_ids=true, to_apply=%region_44.45 | all-reduce | flops 9600 | bytes 76800 | tf_op jit(solution)/shard_map/psum | solution.py:317
  1200.3 285.2 %all-reduce.12.cloned.1.call-done = (bf16[640,320]{0,1:T(8,128)(2,1)}, bf16[640,320]{0,1:T(8,128)(2,1)}, bf16[640,320]{0,1:T(8,128)(2,1)}, bf16[640,320]{0,1:T(8...) async-done(((bf16[640,320]{0,1:T(8,128)(2,1)}, ...) | async-done | bytes 9830416 | tf_op jit(solution)/shard_map/psum | solution.py:305
  (570 shorter events, 367.1 us)
Async XLA Ops:
  7.2 61.0 %all-gather.13.cloned.1.call-start = ((), (), s32[]{:S(2)}) async-start(), calls=%async_computation.17 | async-start | bytes 1638400 | tf_op jit(solution)/shard_map/all_gather | solution.py:90
  10.3 144.1 %copy-start.74 = (f32[1280]{0:T(1024)}, f32[1280]{0:T(1024)S(1)}, u32[]{:S(2)}) copy-start(f32[1280]{0:T(1024)S(1)} %convert_element_type.413) | copy-start | bytes 15364
  10.8 143.6 %copy-start.76 = (f32[1280]{0:T(1024)}, f32[1280]{0:T(1024)S(1)}, u32[]{:S(2)}) copy-start(f32[1280]{0:T(1024)S(1)} %convert_element_type.414) | copy-start | bytes 15364
  27.2 67.9 %all-gather.11.cloned.1.call-start = ((), (), s32[]{:S(2)}) async-start(), calls=%async_computation.16 | async-start | bytes 1638400 | tf_op jit(solution)/shard_map/all_gather | solution.py:91
  42.4 105.1 %all-gather.23.cloned.1.call-start = ((), (), s32[]{:S(2)}) async-start(), calls=%async_computation.30 | async-start | bytes 6553600 | tf_op jit(solution)/shard_map/all_gather | solution.py:121
  107.7 82.4 %all-gather.21.cloned.1.call-start = ((), (), s32[]{:S(2)}) async-start(), calls=%async_computation.21 | async-start | bytes 1638400 | tf_op jit(solution)/shard_map/all_gather | solution.py:90
  108.3 46.2 %copy-start.80 = (f32[512]{0:T(512)}, f32[512]{0:T(512)S(1)}, u32[]{:S(2)}) copy-start(f32[512]{0:T(512)S(1)} %broadcast_multiply_fusion.1) | copy-start | bytes 6148
  157.5 66.3 %all-gather.19.cloned.1.call-start = ((), (), s32[]{:S(2)}) async-start(), calls=%async_computation.20 | async-start | bytes 1638400 | tf_op jit(solution)/shard_map/all_gather | solution.py:91
  160.2 117.2 %all-gather.25.cloned.1.call-start = ((), (), s32[]{:S(2)}) async-start(), calls=%async_computation.31 | async-start | bytes 6553600 | tf_op jit(solution)/shard_map/all_gather | solution.py:121
  237.8 87.6 %all-gather.15.cloned.1.call-start = ((), (), s32[]{:S(2)}) async-start(), calls=%async_computation.18 | async-start | bytes 4915200 | tf_op jit(solution)/shard_map/all_gather | solution.py:69
  238.5 134.8 %all-gather.17.cloned.1.call-start = ((), (), s32[]{:S(2)}) async-start(), calls=%async_computation.19 | async-start | bytes 4915200 | tf_op jit(solution)/shard_map/all_gather | solution.py:70
  239.3 213.6 %all-reduce.10.cloned.1.call-start = ((), (), s32[]{:S(2)}) async-start(), calls=%async_computation.41 | async-start | bytes 5242880 | tf_op jit(solution)/shard_map/psum | solution.py:171
  240.8 97.0 %copy-start.96 = (f32[1280]{0:T(1024)}, f32[1280]{0:T(1024)S(1)}, u32[]{:S(2)}) copy-start(f32[1280]{0:T(1024)S(1)} %convert_element_type.431) | copy-start | bytes 15364
  392.8 236.7 %reduce-scatter.37.cloned.1.call-start = ((), (), s32[]{:S(2)}) async-start(), calls=%async_computation.24 | async-start | bytes 1638400 | tf_op jit(solution)/shard_map/reduce_scatter | solution.py:229
  532.2 100.8 %reduce-scatter.39.cloned.1.call-start = ((), (), s32[]{:S(2)}) async-start(), calls=%async_computation.25 | async-start | bytes 1638400 | tf_op jit(solution)/shard_map/reduce_scatter | solution.py:232
  541.0 98.1 %reduce-scatter.33.cloned.1.call-start = ((), (), s32[]{:S(2)}) async-start(), calls=%async_computation.22 | async-start | bytes 1638400 | tf_op jit(solution)/shard_map/reduce_scatter | solution.py:229
  607.7 63.8 %reduce-scatter.35.cloned.1.call-start = ((), (), s32[]{:S(2)}) async-start(), calls=%async_computation.23 | async-start | bytes 1638400 | tf_op jit(solution)/shard_map/reduce_scatter | solution.py:232
  611.6 103.1 %reduce-scatter.63.cloned.1.call-start = ((), (), s32[]{:S(2)}) async-start(), calls=%async_computation.39 | async-start | bytes 1474560
  615.4 101.3 %reduce-scatter.61.cloned.1.call-start = ((), (), s32[]{:S(2)}) async-start(), calls=%async_computation.38 | async-start | bytes 1474560
  621.2 114.5 %reduce-scatter.51.cloned.1.call-start = ((), (), s32[]{:S(2)}) async-start(), calls=%async_computation.33 | async-start | bytes 1474560
  626.2 131.3 %reduce-scatter.49.cloned.1.call-start = ((), (), s32[]{:S(2)}) async-start(), calls=%async_computation.32 | async-start | bytes 1474560
  629.5 149.8 %reduce-scatter.55.cloned.1.call-start = ((), (), s32[]{:S(2)}) async-start(), calls=%async_computation.35 | async-start | bytes 1474560
  633.0 168.3 %reduce-scatter.59.cloned.1.call-start = ((), (), s32[]{:S(2)}) async-start(), calls=%async_computation.37 | async-start | bytes 1474560
  636.4 186.7 %reduce-scatter.53.cloned.1.call-start = ((), (), s32[]{:S(2)}) async-start(), calls=%async_computation.34 | async-start | bytes 1474560
  642.5 32.4 %copy-start.97 = (f32[1280]{0:T(1024)S(1)}, f32[1280]{0:T(1024)}, u32[]{:S(2)}) copy-start(f32[1280]{0:T(1024)} %copy-done.96) | copy-start | bytes 15364
  642.5 202.6 %reduce-scatter.57.cloned.1.call-start = ((), (), s32[]{:S(2)}) async-start(), calls=%async_computation.36 | async-start | bytes 1474560
  674.9 218.0 %reduce-scatter.41.cloned.1.call-start = ((), (), s32[]{:S(2)}) async-start(), calls=%async_computation.26 | async-start | bytes 4915200 | tf_op jit(solution)/shard_map/reduce_scatter | solution.py:297
  680.4 260.1 %reduce-scatter.43.cloned.1.call-start = ((), (), s32[]{:S(2)}) async-start(), calls=%async_computation.27 | async-start | bytes 4915200 | tf_op jit(solution)/shard_map/reduce_scatter | solution.py:297
  686.0 301.5 %reduce-scatter.45.cloned.1.call-start = ((), (), s32[]{:S(2)}) async-start(), calls=%async_computation.28 | async-start | bytes 4915200 | tf_op jit(solution)/shard_map/reduce_scatter | solution.py:300
  691.6 343.1 %reduce-scatter.47.cloned.1.call-start = ((), (), s32[]{:S(2)}) async-start(), calls=%async_computation.29 | async-start | bytes 4915200 | tf_op jit(solution)/shard_map/reduce_scatter | solution.py:300
  697.1 442.6 %all-reduce.8.cloned.1.call-start = ((), (), s32[]{:S(2)}) async-start(), calls=%async_computation.40 | async-start | bytes 10485760 | tf_op jit(solution)/shard_map/psum | solution.py:142
  714.5 771.0 %all-reduce.12.cloned.1.call-start = ((), (), s32[]{:S(2)}) async-start(), calls=%async_computation.42 | async-start | bytes 19660800 | tf_op jit(solution)/shard_map/psum | solution.py:305
  (137 other events, 459.2 us)
Sparse Core Ops, SparseCore 0:
  27.3 33.9 all-gather.12
  63.5 31.5 all-gather.10
  107.8 39.5 all-gather.22
  157.6 32.5 all-gather.20
  192.1 31.6 all-gather.18
  237.9 39.5 all-gather.24
  279.0 46.3 all-gather.14
  327.0 46.3 all-gather.16
  392.9 59.9 all-reduce.9
  532.3 31.4 reduce-scatter.36
  566.7 30.0 reduce-scatter.38
  607.8 31.2 reduce-scatter.32
  641.4 30.0 reduce-scatter.34
  673.6 18.3 reduce-scatter.62
  694.1 19.6 reduce-scatter.60
  715.9 19.6 reduce-scatter.50
  737.8 19.6 reduce-scatter.48
  759.6 19.6 reduce-scatter.54
  781.6 19.6 reduce-scatter.58
  803.4 19.6 reduce-scatter.52
  825.4 19.6 reduce-scatter.56
  847.9 44.8 reduce-scatter.40
  895.6 44.8 reduce-scatter.42
  942.6 44.8 reduce-scatter.44
  989.8 44.8 reduce-scatter.46
  1037.1 102.5 all-reduce.7
  1145.0 340.4 all-reduce.11
